TPU v7x, 128 devices: a whole 4x4x4 slice. The times are simulated.
128 devices in a mesh: dp: 8 (over z, core), expert: 16 (over y, x).
Axes of the slice: x: 4, y: 4, z: 4, core: 2. Of those that a mesh axis runs over, the one named last changes fastest.
Arguments:
- inputs: bfloat16 [16384, 2048], P(('dp', 'expert')), may hold values from -6 to 6
- out_grad: bfloat16 [16384, 2048], P(('dp', 'expert')), may hold values from -6 to 6
- combine: float32 [16384, 8], P(('dp', 'expert')), may hold values from 0 to 1, as said below
- routes: int32 [16384, 8], P(('dp', 'expert')), may hold values from 0 to 63, all different within a row; in each aligned block of 128 rows (0 to 127, 128 to 255, ...) at most 24 rows name the same one
- saved_hidden: bfloat16 [8, 64, 16, 24, 768], P('dp', 'expert'), may hold values from -6 to 6
- down_weight: bfloat16 [64, 2048, 768], P('expert'), may hold values from -0.21875 to 0.21875
- router_weight: bfloat16 [64, 2048], replicated, may hold values from -0.125 to 0.125
Outputs:
- hidden_grad: bfloat16 [8, 64, 16, 24, 768], P('dp', 'expert')
- down_grad: bfloat16 [64, 2048, 768], P('expert', 'dp')
- input_grad: bfloat16 [16384, 2048], P(('dp', 'expert'))
- router_grad: float32 [64, 2048], replicated
Inputs may be any that keep to these rules, and one draw needn't show every extreme that they name: `routes`: each token names 8 different experts; among the 128 tokens of one device no expert is named by more than 24 tokens, a bound that some block reaches. `combine`: each token's 8 weights are positive and sum to one.
All inputs are finite; a program needn't handle non-finite values.
Results may differ from a plain program's by a relative error of at most 0.017.
Values may be sent and summed in bfloat16 or wider, within the bound.
A program may use at most 128 MiB of HBM per device.

v0:
```python
import jax
import jax.numpy as jnp
from jax import lax
from jax.sharding import PartitionSpec as P


def make_marks(block_routes, total_experts):
    return block_routes[:, :, None] == jnp.arange(total_experts, dtype=jnp.int32)[None, None, :]


def slot_positions(route_marks):
    counts = jnp.sum(route_marks.astype(jnp.bfloat16), axis=1)
    token_order = jnp.arange(route_marks.shape[0], dtype=jnp.int32)
    earlier = (token_order[None, :] < token_order[:, None]).astype(jnp.bfloat16)
    before = jnp.dot(earlier, counts, preferred_element_type=jnp.float32)
    picked = jnp.sum(jnp.where(route_marks, before[:, None, :], 0.0), axis=2)
    return picked.astype(jnp.int32)


def pack_rows(scaled, lane_index, owner_slot, positions, local_experts, groups, capacity):
    width = scaled.shape[-1]
    flat_index = (owner_slot * groups + lane_index) * capacity + positions
    zero_rows = jnp.zeros((local_experts * groups * capacity, width), jnp.bfloat16)
    filled = zero_rows.at[flat_index.reshape(-1)].set(scaled.reshape(-1, width))
    return filled.reshape(local_experts, groups, capacity, width)


def local(inputs, out_grad, combine, routes, saved_hidden, down_weight, router_weight):
    token_count, width = out_grad.shape
    local_experts = down_weight.shape[0]
    total_experts = router_weight.shape[0]
    groups = lax.axis_size("expert")
    capacity = saved_hidden.shape[3]
    hidden_width = saved_hidden.shape[4]
    route_marks = make_marks(routes, total_experts)
    positions = slot_positions(route_marks)
    owner_dev = routes // local_experts
    owner_slot = routes % local_experts
    scaled = (combine[:, :, None] * out_grad[:, None, :].astype(jnp.float32)).astype(jnp.bfloat16)
    packed = pack_rows(scaled, owner_dev, owner_slot, positions, local_experts, groups, capacity)
    received = lax.all_to_all(packed, "expert", split_axis=1, concat_axis=1, tiled=True)
    hidden_local = saved_hidden[0]
    products_list = []
    hidden_list = []
    weight_terms = []
    for expert in range(local_experts):
        slot_rows = received[expert].reshape(groups * capacity, width)
        slot_acts = hidden_local[expert].reshape(groups * capacity, hidden_width)
        weight = down_weight[expert]
        recomputed = lax.dot_general(
            slot_acts, weight, (((1,), (1,)), ((), ())), preferred_element_type=jnp.float32
        )
        products_list.append(jnp.sum(recomputed * slot_rows.astype(jnp.float32), axis=1))
        hidden_list.append(
            jnp.dot(slot_rows, weight, preferred_element_type=jnp.float32).astype(jnp.bfloat16)
        )
        weight_terms.append(
            lax.dot_general(
                slot_rows, slot_acts, (((0,), (0,)), ((), ())), preferred_element_type=jnp.float32
            )
        )
    down_grad = lax.psum_scatter(
        jnp.stack(weight_terms).astype(jnp.bfloat16), "dp", scatter_dimension=1, tiled=True
    )
    hidden_grad = jnp.stack(hidden_list).reshape(1, local_experts, groups, capacity, hidden_width)
    slot_products = jnp.stack(products_list).reshape(local_experts, groups, capacity)
    returned = lax.all_to_all(slot_products, "expert", split_axis=1, concat_axis=1, tiled=True)
    pair_index = (owner_slot * groups + owner_dev) * capacity + positions
    pair_sums = returned.reshape(-1)[pair_index]
    logit_grad = pair_sums - combine * jnp.sum(pair_sums, axis=1, keepdims=True)
    dense_grad = jnp.sum(jnp.where(route_marks, logit_grad[:, :, None], 0.0), axis=1).astype(
        jnp.bfloat16
    )
    input_grad = jnp.dot(dense_grad, router_weight, preferred_element_type=jnp.float32).astype(
        jnp.bfloat16
    )
    router_part = lax.dot_general(
        dense_grad, inputs, (((0,), (0,)), ((), ())), preferred_element_type=jnp.float32
    )
    router_grad = lax.psum(router_part, ("dp", "expert"))
    return (hidden_grad, down_grad, input_grad, router_grad)


def solution(mesh):
    placed = (
        P(("dp", "expert"), None),
        P(("dp", "expert"), None),
        P(("dp", "expert"), None),
        P(("dp", "expert"), None),
        P("dp", "expert", None, None, None),
        P("expert", None, None),
        P(),
    )
    return jax.shard_map(
        local,
        mesh=mesh,
        in_specs=placed,
        out_specs=(
            P("dp", "expert", None, None, None),
            P("expert", "dp", None),
            P(("dp", "expert"), None),
            P(),
        ),
        check_vma=False,
    )
```

profile of v0, /device:TPU:1, one launch (start us, length us, event | category | flops | bytes accessed | tf_op | source)
XLA Modules:
  0.0 366.2 jit_solution(16921963926218966697)
XLA Ops:
  8.0 0.8 fusion.55
  8.9 0.7 select_reduce_fusion.1
  9.7 0.7 compare_select_fusion.1
  10.6 0.8 copy.46
  11.5 1.1 convert_element_type.50
  12.6 10.6 %scatter_custom_fusion = bf16[1536,2048]{1,0:T(8,128)(2,1)} fusion(s32[1024]{0:T(1024)S(1)} %bitcast.110, f32[128,2048]{1,0:T(8,128)S(1)} %convert_element_type.50, f32[1024]{0:T(1024)S(1)} %mul.48, bf16[]{:T(256)} %constant.31.clone.1), kind=kCustom, calls=%fused_computation.5 | custom fusion | flops 4194304 | bytes 7344130 | tf_op jit(solution)/shard_map/scatter | solution.py:24
  23.2 6.6 %copy.47 = bf16[4,16,24,2048]{3,2,0,1:T(8,128)(2,1)} copy(bf16[4,16,24,2048]{3,2,1,0:T(8,128)(2,1)} %bitcast.85) | data formatting | bytes 12582912 | tf_op jit(solution)/shard_map/reshape | solution.py:25
  29.8 7.8 %all-to-all-start = ((bf16[4,16,24,2048]{3,2,0,1:T(8,128)(2,1)}), bf16[4,16,24,2048]{3,2,0,1:T(8,128)(2,1)}, u32[]{:S(2)}, u32[]{:S(2)}) async-start(bf16[4,16,24,2048]{3,2,0,1:T(8,128)(2,1)} %copy.47), calls=%async_computation | async-start | bytes 12582912 | tf_op jit(solution)/shard_map/all_to_all | solution.py:41
  37.8 1.2 fusion.70
  39.0 90.8 %all-to-all-done = bf16[4,16,24,2048]{3,2,0,1:T(8,128)(2,1)} async-done(((bf16[4,16,24,2048]{3,2,0,1:T(8,128)(2,1)}), bf16[4,16,24,2048]{3,2,0,1:T(8,128)(2,1)}, u32[]{:S(2)}, u32[]{:S(2)}) %all-to-all-start) | async-done | bytes 6291488 | tf_op jit(solution)/shard_map/all_to_all | solution.py:41
  129.9 4.8 %fusion.69 = (bf16[1,16,24,2048]{3,2,0,1:T(8,128)(2,1)S(1)}, bf16[1,16,24,2048]{3,2,0,1:T(8,128)(2,1)}, bf16[1,16,24,2048]{3,2,0,1:T(8,128)(2,1)S(1)}, bf16[1,16,24,2048]{3,2,0,1:T(8,128)(2,1)S(1)}) fusion(bf16[4,16,24,2048]{3,2,0,1:T(8,128)(2,1)} %all-to-all-done), kind=kLoop, calls=%fused_computation.80 | loop fusion | bytes 12582912 | tf_op jit(solution)/shard_map/slice | solution.py:47
  134.7 3.5 fusion.23
  138.2 3.6 multiply_reduce_fusion.2
  141.9 1.5 multiply_reduce_fusion.1
  143.4 3.5 fusion.24
  146.9 1.5 multiply_reduce_fusion.3
  148.4 3.5 fusion.22
  152.2 3.9 %multiply_reduce_fusion = f32[384]{0:T(512)S(1)} fusion(bf16[384,2048]{1,0:T(8,128)(2,1)} %bitcast.95, bf16[384,768]{1,0:T(8,128)(2,1)S(1)} %bitcast.98, bf16[4,2048,768]{2,1,0:T(8,128)(2,1)} %param.12), kind=kOutput, calls=%fused_computation.28 | convolution fusion | flops 1210318464 | bytes 5309952 | tf_op jit(solution)/shard_map/dot_general | solution.py:50
  156.9 5.4 %all-to-all-start.1 = ((f32[4,16,24]{2,0,1:T(4,128)}), f32[4,16,24]{2,0,1:T(4,128)S(1)}, u32[]{:S(2)}, u32[]{:S(2)}) async-start(f32[4,16,24]{2,0,1:T(4,128)} %pad_maximum_fusion.2), calls=%async_computation.2 | async-start | bytes 65536 | tf_op jit(solution)/shard_map/all_to_all | solution.py:67
  162.6 4.9 %fusion.25 = bf16[1,2048,768]{2,1,0:T(8,128)(2,1)} fusion(bf16[384,2048]{1,0:T(8,128)(2,1)} %bitcast.96, bf16[384,768]{1,0:T(8,128)(2,1)S(1)} %bitcast.99), kind=kOutput, calls=%fused_computation.36 | convolution fusion | flops 1209532416 | bytes 5308416 | tf_op jit(solution)/shard_map/dot_general | solution.py:58
  167.5 1.3 all-to-all-done.1
  168.8 6.2 %gather_fusion = f32[1024]{0:T(1024)S(1)} fusion(f32[1536]{0:T(1024)S(1)} %reshape.84, s32[1024]{0:T(1024)S(1)} %broadcast_clamp_fusion), kind=kCustom, calls=%fused_computation | custom fusion | bytes 12288 | tf_op jit(solution)/shard_map/gather | solution.py:69
  175.4 1.0 fusion.71
  176.5 10.7 %pad_maximum_fusion = bf16[4,2048,768]{2,1,0:T(8,128)(2,1)} fusion(bf16[1,2048,768]{2,1,0:T(8,128)(2,1)} %fusion.25, bf16[1,2048,768]{2,1,0:T(8,128)(2,1)} %fusion.24, bf16[1,2048,768]{2,1,0:T(8,128)(2,1)} %fusion.23, bf16[1,2048,768]{2,1,0:T(8,128)(2,1)} %fusion.22), kind=kLoop, calls=%fused_computation.2 | loop fusion | flops 18874368 | bytes 25165824 | tf_op jit(solution)/shard_map/stack | solution.py:63
  187.2 3.9 %fusion.51 = bf16[384,768]{1,0:T(8,128)(2,1)S(1)} fusion(bf16[384,2048]{1,0:T(8,128)(2,1)} %bitcast.97, bf16[4,2048,768]{2,1,0:T(8,128)(2,1)} %param.12), kind=kOutput, calls=%fused_computation.50 | convolution fusion | flops 1208254464 | bytes 5308416 | tf_op jit(solution)/shard_map/dot_general | solution.py:55
  191.1 3.4 fusion.42
  194.6 3.3 fusion.48
  197.9 4.1 %fusion.45 = bf16[384,768]{1,0:T(8,128)(2,1)S(1)} fusion(bf16[384,2048]{1,0:T(8,128)(2,1)S(1)} %bitcast.88, bf16[4,2048,768]{2,1,0:T(8,128)(2,1)} %param.12), kind=kOutput, calls=%fused_computation.48 | convolution fusion | flops 1208254464 | bytes 5308416 | tf_op jit(solution)/shard_map/dot_general | solution.py:55
  202.0 1.7 pad_maximum_fusion.1
  203.7 1.1 convolution_convert_fusion.4
  204.9 152.0 %all-reduce.2.cloned.1.call-done = f32[64,2048]{1,0:T(8,128)} async-done(((f32[64,2048]{1,0:T(8,128)}), f32[64,2048]{1,0:T(8,128)}) %all-reduce.2.cloned.1.call-update) | async-done | bytes 524304 | tf_op jit(solution)/shard_map/psum | solution.py:80
  356.9 1.9 copy.52
  (56 shorter events, 2.5 us)
Async XLA Ops:
  8.0 167.4 %copy-start = (bf16[128,2048]{1,0:T(8,128)(2,1)S(1)}, bf16[128,2048]{1,0:T(8,128)(2,1)}, u32[]{:S(2)}) copy-start(bf16[128,2048]{1,0:T(8,128)(2,1)} %param.7) | copy-start | bytes 1572868
  29.8 8.0 %copy-start.1 = (bf16[1,4,16,24,768]{4,3,2,1,0:T(8,128)(2,1)S(1)}, bf16[1,4,16,24,768]{4,3,2,1,0:T(8,128)(2,1)}, u32[]{:S(2)}) copy-start(bf16[1,4,16,24,768]{4,3,2,1,0:T(8,128)(2,1)} %param.11) | copy-start | bytes 7077892
  29.8 100.1 %all-to-all-start = ((bf16[4,16,24,2048]{3,2,0,1:T(8,128)(2,1)}), bf16[4,16,24,2048]{3,2,0,1:T(8,128)(2,1)}, u32[]{:S(2)}, u32[]{:S(2)}) async-start(bf16[4,16,24,2048]{3,2,0,1:T(8,128)(2,1)} %copy.47), calls=%async_computation | async-start | bytes 12582912 | tf_op jit(solution)/shard_map/all_to_all | solution.py:41
  39.0 95.7 %copy-start.8 = (bf16[1,1,16,24,768]{4,3,2,1,0:T(8,128)(2,1)S(1)}, bf16[1,1,16,24,768]{4,3,2,1,0:T(8,128)(2,1)}, u32[]{:S(2)}) copy-start(bf16[1,1,16,24,768]{4,3,2,1,0:T(8,128)(2,1)} %get-tuple-element.11) | copy-start | bytes 1769476
  129.9 11.9 %slice-start = ((s8[12582912]{0:T(1024)(128)(4,1)}), s8[4194304]{0:T(1024)(128)(4,1)S(1)}, s32[]{:S(2)}) async-start(s8[12582912]{0:T(1024)(128)(4,1)} %bitcast.111), calls=%async_computation.5 | async-start | bytes 8388608
  129.9 11.9 %slice-start.1 = ((s8[12582912]{0:T(1024)(128)(4,1)}), s8[4194304]{0:T(1024)(128)(4,1)S(1)}, s32[]{:S(2)}) async-start(s8[12582912]{0:T(1024)(128)(4,1)} %bitcast.111), calls=%async_computation.6 | async-start | bytes 8388608
  134.7 8.7 %copy-start.2 = (bf16[1,16,24,2048]{3,2,0,1:T(8,128)(2,1)}, bf16[1,16,24,2048]{3,2,0,1:T(8,128)(2,1)S(1)}, u32[]{:S(2)}) copy-start(bf16[1,16,24,2048]{3,2,0,1:T(8,128)(2,1)S(1)} %get-tuple-element.8) | copy-start | bytes 4718596
  134.7 13.7 %copy-start.4 = (bf16[1,16,24,2048]{3,2,0,1:T(8,128)(2,1)}, bf16[1,16,24,2048]{3,2,0,1:T(8,128)(2,1)S(1)}, u32[]{:S(2)}) copy-start(bf16[1,16,24,2048]{3,2,0,1:T(8,128)(2,1)S(1)} %get-tuple-element.6) | copy-start | bytes 4718596
  138.2 3.6 copy-start.7
  138.2 3.6 slice-start.2
  143.4 3.5 copy-start.6
  156.9 11.8 %all-to-all-start.1 = ((f32[4,16,24]{2,0,1:T(4,128)}), f32[4,16,24]{2,0,1:T(4,128)S(1)}, u32[]{:S(2)}, u32[]{:S(2)}) async-start(f32[4,16,24]{2,0,1:T(4,128)} %pad_maximum_fusion.2), calls=%async_computation.2 | async-start | bytes 65536 | tf_op jit(solution)/shard_map/all_to_all | solution.py:67
  162.3 194.6 %all-reduce.2.cloned.1.call-start = ((), (), s32[]{:S(2)}) async-start(), calls=%async_computation.4 | async-start | bytes 1048576 | tf_op jit(solution)/shard_map/psum | solution.py:80
  168.8 6.5 %copy-start.11 = (f32[128,8]{0,1:T(8,128)S(1)}, f32[128,8]{0,1:T(8,128)}, u32[]{:S(2)}) copy-start(f32[128,8]{0,1:T(8,128)} %param.9) | copy-start | bytes 12292
  168.8 6.5 %copy-start.10 = (s32[128,8]{0,1:T(8,128)S(1)}, s32[128,8]{0,1:T(8,128)}, u32[]{:S(2)}) copy-start(s32[128,8]{0,1:T(8,128)} %param.10) | copy-start | bytes 12292
  176.4 180.5 %reduce-scatter.2.cloned.1.call-start = ((), (), s32[]{:S(2)}) async-start(), calls=%async_computation.3 | async-start | bytes 14155776 | tf_op jit(solution)/shard_map/reduce_scatter | solution.py:62
  187.2 3.9 %copy-start.5 = (bf16[1,16,24,2048]{3,2,0,1:T(8,128)(2,1)S(1)}, bf16[1,16,24,2048]{3,2,0,1:T(8,128)(2,1)}, u32[]{:S(2)}) copy-start(bf16[1,16,24,2048]{3,2,0,1:T(8,128)(2,1)} %copy-done.4) | copy-start | bytes 4718596
  191.1 3.5 copy-start.3
  202.0 1.7 copy-start.9
Sparse Core Ops, SparseCore 0:
  176.5 180.2 all-reduce.1
Sparse Core Ops, SparseCore 1:
  187.3 75.3 reduce-scatter.1
where the time goes:
time: 367 us; the launch traced here: 366 us
  waiting for transfers between devices  244 us (66%)
  matrix products  43 us (12%)
  other arithmetic  27.2 us (7%)
  local copies, waits for them, and re-layouts  22.6 us (6%)
  between operations  15.8 us (4%)
  starting transfers between devices  13.5 us (4%)
    psum x1, waiting for transfers between devices, local(): router_grad = lax.psum(router_part, ('dp', 'expert'))  152 us
    all_to_all x1, waiting for transfers between devices, local(): lax.all_to_all(packed, 'expert', split_axis=1, concat_axis=1, tiled=True)  90.8 us
    dot_general x4, matrix products, local(): lax.dot_general(slot_rows, slot_acts, (((0,), (0,)), ((), ())), preferred...  15.5 us
    dot_general x4, matrix products, local(): jnp.dot(slot_rows, weight, preferred_element_type=jnp.float32)  14.8 us
    another operation x1, other arithmetic, local(): jnp.stack(weight_terms).astype(jnp.bfloat16)  10.7 us
    scatter x1, other arithmetic, pack_rows(): filled = zero_rows.at[flat_index.reshape(-1)].set(scaled.reshape(-1, width))  10.6 us
    dot_general x4, matrix products, local(): lax.dot_general(slot_acts, weight, (((1,), (1,)), ((), ())), preferred_el...  10.5 us
    all_to_all x1, starting transfers between devices, local(): lax.all_to_all(packed, 'expert', split_axis=1, concat_axis=1, tiled=True)  7.77 us
  transfers between devices with their start and end apart: 4, of which 3 were waited for; matrix products, arithmetic and copies ran while one was open for 9% of the time, Pallas kernels for 0%

commit v1 on v0

--- a/solution.py
+++ b/solution.py
@@ -77,7 +77,7 @@
     router_part = lax.dot_general(
         dense_grad, inputs, (((0,), (0,)), ((), ())), preferred_element_type=jnp.float32
     )
-    router_grad = lax.psum(router_part, ("dp", "expert"))
+    router_grad = lax.psum(lax.psum(router_part, "dp"), "expert")
     return (hidden_grad, down_grad, input_grad, router_grad)
 
 

time: 367 us -> 411 us (1.12)
  waiting for transfers between devices: 244 us -> 285 us
  matrix products: 43 us -> 47.8 us
    reduce_scatter x1, waiting for transfers between devices: 0.01 us -> 75.6 us  [local(): lax.psum_scatter(jnp.stack(weight_terms).astype(jnp.bfloat16), 'dp', scat...]
    psum x1 -> x2, waiting for transfers between devices: 152 us -> 117 us  [local(): router_grad = lax.psum(lax.psum(router_part, 'dp'), 'expert')]
    dot_general x4, matrix products: 10.5 us -> 14.7 us  [local(): lax.dot_general(slot_acts, weight, (((1,), (1,)), ((), ())), preferred_el...]
  transfers between devices with their start and end apart: 4 -> 5, of which waited for: 3 -> 5; matrix products, arithmetic and copies ran while one was open for 9% -> 9% of each run, Pallas kernels for 0% -> 0%
where the time goes in v1:
time: 411 us
  waiting for transfers between devices  285 us (69%)
  matrix products  47.8 us (12%)
  other arithmetic  27.2 us (7%)
  local copies, waits for them, and re-layouts  23.2 us (6%)
  between operations  14 us (3%)
  starting transfers between devices  13.5 us (3%)
    psum x2, waiting for transfers between devices, local(): router_grad = lax.psum(lax.psum(router_part, 'dp'), 'expert')  117 us
    all_to_all x1, waiting for transfers between devices, local(): lax.all_to_all(packed, 'expert', split_axis=1, concat_axis=1, tiled=True)  90.8 us
    reduce_scatter x1, waiting for transfers between devices, local(): lax.psum_scatter(jnp.stack(weight_terms).astype(jnp.bfloat16), 'dp', scat...  75.6 us
    dot_general x4, matrix products, local(): lax.dot_general(slot_rows, slot_acts, (((0,), (0,)), ((), ())), preferred...  16.9 us
    dot_general x4, matrix products, local(): lax.dot_general(slot_acts, weight, (((1,), (1,)), ((), ())), preferred_el...  14.7 us
    dot_general x4, matrix products, local(): jnp.dot(slot_rows, weight, preferred_element_type=jnp.float32)  14 us
    another operation x1, other arithmetic, local(): jnp.stack(weight_terms).astype(jnp.bfloat16)  10.7 us
    scatter x1, other arithmetic, pack_rows(): filled = zero_rows.at[flat_index.reshape(-1)].set(scaled.reshape(-1, width))  10.6 us
  transfers between devices with their start and end apart: 5, of which 5 were waited for; matrix products, arithmetic and copies ran while one was open for 9% of the time, Pallas kernels for 0%

profile of v1, /device:TPU:1, one launch (start us, length us, event | category | flops | bytes accessed | tf_op | source)
XLA Modules:
  0.0 410.6 jit_solution(15486615265287168678)
XLA Ops:
  7.2 0.8 fusion.55
  9.8 0.8 copy.46
  10.6 1.1 convert_element_type.50
  11.8 10.6 %scatter_custom_fusion = bf16[1536,2048]{1,0:T(8,128)(2,1)} fusion(s32[1024]{0:T(1024)S(1)} %bitcast.110, f32[128,2048]{1,0:T(8,128)S(1)} %convert_element_type.50, f32[1024]{0:T(1024)S(1)} %mul.48, bf16[]{:T(256)} %constant.31.clone.1), kind=kCustom, calls=%fused_computation.5 | custom fusion | flops 4194304 | bytes 7344130 | tf_op jit(solution)/shard_map/scatter | solution.py:24
  22.4 6.6 %copy.47 = bf16[4,16,24,2048]{3,2,0,1:T(8,128)(2,1)} copy(bf16[4,16,24,2048]{3,2,1,0:T(8,128)(2,1)} %bitcast.85) | data formatting | bytes 12582912 | tf_op jit(solution)/shard_map/reshape | solution.py:25
  29.0 7.8 %all-to-all-start = ((bf16[4,16,24,2048]{3,2,0,1:T(8,128)(2,1)}), bf16[4,16,24,2048]{3,2,0,1:T(8,128)(2,1)}, u32[]{:S(2)}, u32[]{:S(2)}) async-start(bf16[4,16,24,2048]{3,2,0,1:T(8,128)(2,1)} %copy.47), calls=%async_computation | async-start | bytes 12582912 | tf_op jit(solution)/shard_map/all_to_all | solution.py:41
  37.0 1.2 fusion.70
  38.2 90.8 %all-to-all-done = bf16[4,16,24,2048]{3,2,0,1:T(8,128)(2,1)} async-done(((bf16[4,16,24,2048]{3,2,0,1:T(8,128)(2,1)}), bf16[4,16,24,2048]{3,2,0,1:T(8,128)(2,1)}, u32[]{:S(2)}, u32[]{:S(2)}) %all-to-all-start) | async-done | bytes 6291488 | tf_op jit(solution)/shard_map/all_to_all | solution.py:41
  129.0 5.4 %fusion.69 = (bf16[1,16,24,2048]{3,2,0,1:T(8,128)(2,1)}, bf16[1,16,24,2048]{3,2,0,1:T(8,128)(2,1)}, bf16[1,16,24,2048]{3,2,0,1:T(8,128)(2,1)S(1)}, bf16[1,16,24,2048]{3,2,0,1:T(8,128)(2,1)S(1)}) fusion(bf16[4,16,24,2048]{3,2,0,1:T(8,128)(2,1)} %all-to-all-done), kind=kLoop, calls=%fused_computation.80 | loop fusion | bytes 12582912 | tf_op jit(solution)/shard_map/slice | solution.py:47
  134.5 3.5 fusion.23
  138.0 3.5 multiply_reduce_fusion.2
  141.5 3.4 multiply_reduce_fusion.1
  144.9 3.5 fusion.24
  148.6 3.9 multiply_reduce_fusion.3
  152.6 3.9 multiply_reduce_fusion
  157.3 5.4 %all-to-all-start.1 = ((f32[4,16,24]{2,0,1:T(4,128)}), f32[4,16,24]{2,0,1:T(4,128)S(1)}, u32[]{:S(2)}, u32[]{:S(2)}) async-start(f32[4,16,24]{2,0,1:T(4,128)} %pad_maximum_fusion.2), calls=%async_computation.2 | async-start | bytes 65536 | tf_op jit(solution)/shard_map/all_to_all | solution.py:67
  162.7 5.0 %fusion.22 = bf16[1,2048,768]{2,1,0:T(8,128)(2,1)} fusion(bf16[384,2048]{1,0:T(8,128)(2,1)} %bitcast.93, bf16[384,768]{1,0:T(8,128)(2,1)S(1)} %bitcast.101), kind=kOutput, calls=%fused_computation.33 | convolution fusion | flops 1209532416 | bytes 5308416 | tf_op jit(solution)/shard_map/dot_general | solution.py:58
  167.7 1.4 all-to-all-done.1
  169.3 6.2 %gather_fusion = f32[1024]{0:T(1024)S(1)} fusion(f32[1536]{0:T(1024)S(1)} %reshape.84, s32[1024]{0:T(1024)S(1)} %broadcast_clamp_fusion), kind=kCustom, calls=%fused_computation | custom fusion | bytes 12288 | tf_op jit(solution)/shard_map/gather | solution.py:69
  175.8 1.0 fusion.71
  177.1 4.9 %fusion.25 = bf16[1,2048,768]{2,1,0:T(8,128)(2,1)} fusion(bf16[384,2048]{1,0:T(8,128)(2,1)} %bitcast.96, bf16[384,768]{1,0:T(8,128)(2,1)S(1)} %bitcast.99), kind=kOutput, calls=%fused_computation.36 | convolution fusion | flops 1209532416 | bytes 5308416 | tf_op jit(solution)/shard_map/dot_general | solution.py:58
  182.0 56.4 %all-reduce.3.cloned.1.call-done = f32[64,2048]{1,0:T(8,128)} async-done(((f32[64,2048]{1,0:T(8,128)}), f32[64,2048]{1,0:T(8,128)}) %all-reduce.3.cloned.1.call-update) | async-done | bytes 524304 | tf_op jit(solution)/shard_map/psum | solution.py:80
  238.4 10.7 %pad_maximum_fusion = bf16[4,2048,768]{2,1,0:T(8,128)(2,1)} fusion(bf16[1,2048,768]{2,1,0:T(8,128)(2,1)} %fusion.25, bf16[1,2048,768]{2,1,0:T(8,128)(2,1)} %fusion.24, bf16[1,2048,768]{2,1,0:T(8,128)(2,1)} %fusion.23, bf16[1,2048,768]{2,1,0:T(8,128)(2,1)} %fusion.22), kind=kLoop, calls=%fused_computation.2 | loop fusion | flops 18874368 | bytes 25165824 | tf_op jit(solution)/shard_map/stack | solution.py:63
  249.2 3.9 fusion.51
  253.1 3.4 fusion.42
  256.6 3.3 fusion.48
  259.9 3.3 fusion.45
  263.2 1.7 pad_maximum_fusion.1
  264.9 1.1 convolution_convert_fusion.4
  266.0 60.6 %all-reduce.5.cloned.1.call-done = f32[64,2048]{1,0:T(8,128)} async-done(((f32[64,2048]{1,0:T(8,128)}), f32[64,2048]{1,0:T(8,128)}) %all-reduce.5.cloned.1.call-update) | async-done | bytes 524304 | tf_op jit(solution)/shard_map/psum | solution.py:80
  326.6 75.6 %reduce-scatter.2.cloned.1.call-done = bf16[4,256,768]{2,1,0:T(8,128)(2,1)} async-done(((bf16[4,2048,768]{2,1,0:T(8,128)(2,1)}), bf16[4,256,768]{2,1,0:T(8,128)(2,1)}) %reduce-scatter.2.cloned.1.call-update) | async-done | bytes 1572880 | tf_op jit(solution)/shard_map/reduce_scatter | solution.py:62
  402.2 1.9 copy.53
  (50 shorter events, 4.0 us)
Async XLA Ops:
  7.2 168.6 %copy-start = (bf16[128,2048]{1,0:T(8,128)(2,1)S(1)}, bf16[128,2048]{1,0:T(8,128)(2,1)}, u32[]{:S(2)}) copy-start(bf16[128,2048]{1,0:T(8,128)(2,1)} %param.7) | copy-start | bytes 1572868
  29.0 8.0 %copy-start.1 = (bf16[1,4,16,24,768]{4,3,2,1,0:T(8,128)(2,1)S(1)}, bf16[1,4,16,24,768]{4,3,2,1,0:T(8,128)(2,1)}, u32[]{:S(2)}) copy-start(bf16[1,4,16,24,768]{4,3,2,1,0:T(8,128)(2,1)} %param.11) | copy-start | bytes 7077892
  29.0 100.1 %all-to-all-start = ((bf16[4,16,24,2048]{3,2,0,1:T(8,128)(2,1)}), bf16[4,16,24,2048]{3,2,0,1:T(8,128)(2,1)}, u32[]{:S(2)}, u32[]{:S(2)}) async-start(bf16[4,16,24,2048]{3,2,0,1:T(8,128)(2,1)} %copy.47), calls=%async_computation | async-start | bytes 12582912 | tf_op jit(solution)/shard_map/all_to_all | solution.py:41
  38.2 96.3 %copy-start.7 = (bf16[1,1,16,24,768]{4,3,2,1,0:T(8,128)(2,1)S(1)}, bf16[1,1,16,24,768]{4,3,2,1,0:T(8,128)(2,1)}, u32[]{:S(2)}) copy-start(bf16[1,1,16,24,768]{4,3,2,1,0:T(8,128)(2,1)} %get-tuple-element.11) | copy-start | bytes 1769476
  134.5 10.4 %copy-start.2 = (bf16[1,16,24,2048]{3,2,0,1:T(8,128)(2,1)}, bf16[1,16,24,2048]{3,2,0,1:T(8,128)(2,1)S(1)}, u32[]{:S(2)}) copy-start(bf16[1,16,24,2048]{3,2,0,1:T(8,128)(2,1)S(1)} %get-tuple-element.8) | copy-start | bytes 4718596
  138.0 3.5 copy-start.6
  144.9 3.7 copy-start.5
  157.3 11.9 %all-to-all-start.1 = ((f32[4,16,24]{2,0,1:T(4,128)}), f32[4,16,24]{2,0,1:T(4,128)S(1)}, u32[]{:S(2)}, u32[]{:S(2)}) async-start(f32[4,16,24]{2,0,1:T(4,128)} %pad_maximum_fusion.2), calls=%async_computation.2 | async-start | bytes 65536 | tf_op jit(solution)/shard_map/all_to_all | solution.py:67
  162.7 75.7 %all-reduce.3.cloned.1.call-start = ((), (), s32[]{:S(2)}) async-start(), calls=%async_computation.4 | async-start | bytes 1048576 | tf_op jit(solution)/shard_map/psum | solution.py:80
  169.2 6.5 %copy-start.10 = (f32[128,8]{0,1:T(8,128)S(1)}, f32[128,8]{0,1:T(8,128)}, u32[]{:S(2)}) copy-start(f32[128,8]{0,1:T(8,128)} %param.9) | copy-start | bytes 12292
  169.3 6.5 %copy-start.9 = (s32[128,8]{0,1:T(8,128)S(1)}, s32[128,8]{0,1:T(8,128)}, u32[]{:S(2)}) copy-start(s32[128,8]{0,1:T(8,128)} %param.10) | copy-start | bytes 12292
  176.8 149.8 %all-reduce.5.cloned.1.call-start = ((), (), s32[]{:S(2)}) async-start(), calls=%async_computation.5 | async-start | bytes 1048576 | tf_op jit(solution)/shard_map/psum | solution.py:80
  238.4 163.9 %reduce-scatter.2.cloned.1.call-start = ((), (), s32[]{:S(2)}) async-start(), calls=%async_computation.3 | async-start | bytes 14155776 | tf_op jit(solution)/shard_map/reduce_scatter | solution.py:62
  249.2 4.0 copy-start.4
  253.1 3.4 copy-start.3
  263.2 1.7 copy-start.8
Sparse Core Ops, SparseCore 0:
  176.9 61.3 all-reduce.2
  241.9 84.6 all-reduce.4
  329.6 72.5 reduce-scatter.1
